TPU v7x, 128 devices: a whole 4x4x4 slice. The times are simulated.
128 devices in a mesh: dp: 8 (over z, x_hi), ind: 16 (over y, x_lo, core).
Axes of the slice: x: 4 (x_hi: 2, x_lo: 2; x = x_hi * 2 + x_lo), y: 4, z: 4, core: 2. Of those that a mesh axis runs over, the one named last changes fastest.
Arguments:
- factor_rows: bfloat16 [8192, 8192], P('ind'), may hold values from -0.0625 to 0.0625
- diag_inverse: float32 [8192, 512], P('ind'), may hold values from -0.2 to 1.5, as said below
- inducing: float32 [8, 8192], P(None, 'ind'), may hold values from -6 to 6
- data_points: float32 [8, 2048], P(None, 'dp'), may hold values from -6 to 6
- lengthscale: float32 [8], replicated, may hold values from 1.5 to 4
- carried: float32 [8192, 2048], P('ind', 'dp'), may hold values from -4 to 4
- block_order: int32 [16], replicated, may hold values from 0 to 15, each once
- panel_pair: int32 [2], replicated, may hold values from 0 to 15, as said below
Outputs:
- solved: bfloat16 [8192, 2048], P('ind', 'dp')
- gram: float32 [1024, 1024], P('dp')
Inputs may be any that keep to these rules, and one draw needn't show every extreme that they name: `diag_inverse`: each 512 x 512 block is lower triangular with its diagonal between 0.5 and 1.5. `panel_pair`: the two positions differ, and one of them is the last position 15.
All inputs are finite; a program needn't handle non-finite values.
Results may differ from a plain program's by a relative error of at most 0.0095.
Values may be sent and summed in bfloat16 or wider, within the bound.
A program may use at most 64 MiB of HBM per device.

v0:
```python
import jax
import jax.numpy as jnp
from jax import lax
from jax.sharding import PartitionSpec as P


def from_root(block, axis, holder):
    block = jnp.where(lax.axis_index(axis) == holder, block, jnp.zeros_like(block))
    return lax.psum(block, axis)


def on_device(
    factor_rows, diag_inverse, inducing, data_points, lengthscale, carried, block_order, panel_pair
):
    owner_index = lax.axis_index("ind")
    width = diag_inverse.shape[1]
    slot_count = diag_inverse.shape[0] // width
    points = data_points.shape[1]
    block_count = block_order.shape[0]
    distance = jnp.zeros((slot_count * width, points), jnp.float32)
    for feature in range(inducing.shape[0]):
        offset = (inducing[feature][:, None] - data_points[feature][None, :]) / lengthscale[feature]
        distance = distance + offset * offset
    kernel = jnp.exp(-0.5 * distance)
    residual = (kernel - carried).reshape(slot_count, width, points)
    factor_slots = factor_rows.reshape(slot_count, width, block_count * width)
    inverse_slots = diag_inverse.reshape(slot_count, width, width)
    stored_ids = owner_index * slot_count + jnp.arange(slot_count, dtype=jnp.int32)
    positions = jnp.sum(
        jnp.where(
            block_order[None, :] == stored_ids[:, None],
            jnp.arange(block_count, dtype=jnp.int32)[None, :],
            0,
        ),
        axis=1,
    )

    def local_of(stored):
        return jnp.clip(stored - owner_index * slot_count, 0, slot_count - 1)

    def factor_cols(local_slot, index):
        return lax.dynamic_slice_in_dim(
            factor_slots[local_slot], (index * width).astype(jnp.int32), width, 1
        )

    def apply_inverse(local_slot, rows_now):
        return jnp.dot(
            inverse_slots[local_slot],
            rows_now,
            precision=lax.Precision.HIGHEST,
            preferred_element_type=jnp.float32,
        ).astype(jnp.bfloat16)

    def empty_panel():
        return jnp.zeros((width, points), jnp.bfloat16)

    def solve_own(residual, index):
        stored = block_order[index]
        local_slot = local_of(stored)

        def do_solve():
            return apply_inverse(local_slot, residual[local_slot])

        return (
            lax.cond(stored // slot_count == owner_index, do_solve, empty_panel),
            stored // slot_count,
        )

    def update_all(residual, panel_now, index):
        current = residual[0]
        cols_now = factor_cols(0, index)

        def do_update():
            return current - jnp.dot(cols_now, panel_now, preferred_element_type=jnp.float32)

        def keep_rows():
            return current

        updated = [lax.cond(positions[0] > index, do_update, keep_rows)]
        return jnp.stack(updated)

    def record(solved, first_tile, second_tile, panel_now, index):
        stored = block_order[index]
        local_slot = local_of(stored)
        placed = panel_now[None]
        solved = jnp.where(stored // slot_count == owner_index, placed, solved)
        first_tile = jnp.where(index == panel_pair[0], panel_now, first_tile)
        second_tile = jnp.where(index == panel_pair[1], panel_now, second_tile)
        return (solved, first_tile, second_tile)

    solved = jnp.zeros((slot_count, width, points), jnp.bfloat16)
    first_tile = empty_panel()
    second_tile = empty_panel()

    def turn(index, carry):
        residual, solved, first_tile, second_tile = carry
        own_panel, owner = solve_own(residual, index)
        panel_now = from_root(own_panel, "ind", owner)
        solved, first_tile, second_tile = record(solved, first_tile, second_tile, panel_now, index)
        residual = update_all(residual, panel_now, index)
        return (residual, solved, first_tile, second_tile)

    residual, solved, first_tile, second_tile = lax.fori_loop(
        0, block_count, turn, (residual, solved, first_tile, second_tile)
    )
    contract = (((1,), (1,)), ((), ()))
    upper_left = lax.dot_general(
        first_tile, first_tile, contract, preferred_element_type=jnp.float32
    )
    lower_left = lax.dot_general(
        second_tile, first_tile, contract, preferred_element_type=jnp.float32
    )
    lower_right = lax.dot_general(
        second_tile, second_tile, contract, preferred_element_type=jnp.float32
    )
    top_rows = jnp.concatenate([jnp.tril(upper_left), jnp.zeros_like(upper_left)], 1)
    bottom_rows = jnp.concatenate([lower_left, jnp.tril(lower_right)], 1)
    gram_tile = jnp.concatenate([top_rows, bottom_rows], 0)
    scale = 1.0 / (points * lax.axis_size("dp"))
    total = lax.psum(gram_tile.astype(jnp.bfloat16), "dp").astype(jnp.float32)
    share_rows = total.shape[0] // lax.axis_size("dp")
    gram = lax.dynamic_slice_in_dim(total, lax.axis_index("dp") * share_rows, share_rows, 0)
    return (solved.reshape(slot_count * width, points), gram * scale)


def solution(mesh):
    in_specs = (
        P("ind", None),
        P("ind", None),
        P(None, "ind"),
        P(None, "dp"),
        P(),
        P("ind", "dp"),
        P(),
        P(),
    )
    out_specs = (P("ind", "dp"), P("dp", None))
    return jax.shard_map(
        on_device, mesh=mesh, in_specs=in_specs, out_specs=out_specs, check_vma=False
    )
```

profile of v0, /device:TPU:0, one launch (start us, length us, event | category | flops | bytes accessed | tf_op | source)
XLA Modules:
  0.0 2147.9 jit_solution(13899003276891774317)
XLA Ops:
  8.0 1.6 fusion.13
  13.1 6.9 subtract_bitcast_fusion
  19.9 2008.1 %while.22 = (s32[]{:T(128)}, f32[1,512,256]{2,1,0:T(8,128)S(1)}, bf16[1,512,256]{2,1,0:T(8,128)(2,1)S(1)}, bf16[512,256]{1,0:T(8,128)(2,1)S(1)}, bf16[512,256]{1...) while((s32[]{:T(128)}, f32[1,512,256]{2,1,0:T(8,128)S(1)}, ...), condition=%wide.region_7.8_spmd.clone, body=%wide.region_1.7_spmd.clone.sunk | while | flops 940834816 | bytes 7864733 | solution.py:103
  26.8 118.4 %all-reduce.6.cloned.1.call-done = bf16[512,256]{1,0:T(8,128)(2,1)} async-done(((bf16[512,256]{1,0:T(8,128)(2,1)}), bf16[512,256]{1,0:T(8,128)(2,1)}) %all-reduce.6.cloned.1.call-update) | async-done | bytes 262160 | tf_op jit(solution)/shard_map/while/body/eval_jaxpr/psum | solution.py:9
  145.2 1.4 conditional.7
  145.2 1.4 fusion.2
  155.6 115.8 %all-reduce.6.cloned.1.call-done = bf16[512,256]{1,0:T(8,128)(2,1)} async-done(((bf16[512,256]{1,0:T(8,128)(2,1)}), bf16[512,256]{1,0:T(8,128)(2,1)}) %all-reduce.6.cloned.1.call-update) | async-done | bytes 262160 | tf_op jit(solution)/shard_map/while/body/eval_jaxpr/psum | solution.py:9
  271.4 1.4 conditional.7
  271.4 1.4 fusion.2
  281.9 115.8 %all-reduce.6.cloned.1.call-done = bf16[512,256]{1,0:T(8,128)(2,1)} async-done(((bf16[512,256]{1,0:T(8,128)(2,1)}), bf16[512,256]{1,0:T(8,128)(2,1)}) %all-reduce.6.cloned.1.call-update) | async-done | bytes 262160 | tf_op jit(solution)/shard_map/while/body/eval_jaxpr/psum | solution.py:9
  397.7 1.4 conditional.7
  397.7 1.4 fusion.2
  408.1 115.5 %all-reduce.6.cloned.1.call-done = bf16[512,256]{1,0:T(8,128)(2,1)} async-done(((bf16[512,256]{1,0:T(8,128)(2,1)}), bf16[512,256]{1,0:T(8,128)(2,1)}) %all-reduce.6.cloned.1.call-update) | async-done | bytes 262160 | tf_op jit(solution)/shard_map/while/body/eval_jaxpr/psum | solution.py:9
  523.6 1.4 conditional.7
  523.6 1.4 fusion.2
  529.8 2.2 conditional.6
  529.8 2.2 convolution_convert_fusion
  536.2 113.3 %all-reduce.6.cloned.1.call-done = bf16[512,256]{1,0:T(8,128)(2,1)} async-done(((bf16[512,256]{1,0:T(8,128)(2,1)}), bf16[512,256]{1,0:T(8,128)(2,1)}) %all-reduce.6.cloned.1.call-update) | async-done | bytes 262160 | tf_op jit(solution)/shard_map/while/body/eval_jaxpr/psum | solution.py:9
  658.5 119.1 %all-reduce.6.cloned.1.call-done = bf16[512,256]{1,0:T(8,128)(2,1)} async-done(((bf16[512,256]{1,0:T(8,128)(2,1)}), bf16[512,256]{1,0:T(8,128)(2,1)}) %all-reduce.6.cloned.1.call-update) | async-done | bytes 262160 | tf_op jit(solution)/shard_map/while/body/eval_jaxpr/psum | solution.py:9
  786.6 115.8 %all-reduce.6.cloned.1.call-done = bf16[512,256]{1,0:T(8,128)(2,1)} async-done(((bf16[512,256]{1,0:T(8,128)(2,1)}), bf16[512,256]{1,0:T(8,128)(2,1)}) %all-reduce.6.cloned.1.call-update) | async-done | bytes 262160 | tf_op jit(solution)/shard_map/while/body/eval_jaxpr/psum | solution.py:9
  911.5 116.9 %all-reduce.6.cloned.1.call-done = bf16[512,256]{1,0:T(8,128)(2,1)} async-done(((bf16[512,256]{1,0:T(8,128)(2,1)}), bf16[512,256]{1,0:T(8,128)(2,1)}) %all-reduce.6.cloned.1.call-update) | async-done | bytes 262160 | tf_op jit(solution)/shard_map/while/body/eval_jaxpr/psum | solution.py:9
  1037.3 115.8 %all-reduce.6.cloned.1.call-done = bf16[512,256]{1,0:T(8,128)(2,1)} async-done(((bf16[512,256]{1,0:T(8,128)(2,1)}), bf16[512,256]{1,0:T(8,128)(2,1)}) %all-reduce.6.cloned.1.call-update) | async-done | bytes 262160 | tf_op jit(solution)/shard_map/while/body/eval_jaxpr/psum | solution.py:9
  1162.1 116.2 %all-reduce.6.cloned.1.call-done = bf16[512,256]{1,0:T(8,128)(2,1)} async-done(((bf16[512,256]{1,0:T(8,128)(2,1)}), bf16[512,256]{1,0:T(8,128)(2,1)}) %all-reduce.6.cloned.1.call-update) | async-done | bytes 262160 | tf_op jit(solution)/shard_map/while/body/eval_jaxpr/psum | solution.py:9
  1287.3 115.8 %all-reduce.6.cloned.1.call-done = bf16[512,256]{1,0:T(8,128)(2,1)} async-done(((bf16[512,256]{1,0:T(8,128)(2,1)}), bf16[512,256]{1,0:T(8,128)(2,1)}) %all-reduce.6.cloned.1.call-update) | async-done | bytes 262160 | tf_op jit(solution)/shard_map/while/body/eval_jaxpr/psum | solution.py:9
  1412.1 115.5 %all-reduce.6.cloned.1.call-done = bf16[512,256]{1,0:T(8,128)(2,1)} async-done(((bf16[512,256]{1,0:T(8,128)(2,1)}), bf16[512,256]{1,0:T(8,128)(2,1)}) %all-reduce.6.cloned.1.call-update) | async-done | bytes 262160 | tf_op jit(solution)/shard_map/while/body/eval_jaxpr/psum | solution.py:9
  1536.6 115.8 %all-reduce.6.cloned.1.call-done = bf16[512,256]{1,0:T(8,128)(2,1)} async-done(((bf16[512,256]{1,0:T(8,128)(2,1)}), bf16[512,256]{1,0:T(8,128)(2,1)}) %all-reduce.6.cloned.1.call-update) | async-done | bytes 262160 | tf_op jit(solution)/shard_map/while/body/eval_jaxpr/psum | solution.py:9
  1661.4 115.5 %all-reduce.6.cloned.1.call-done = bf16[512,256]{1,0:T(8,128)(2,1)} async-done(((bf16[512,256]{1,0:T(8,128)(2,1)}), bf16[512,256]{1,0:T(8,128)(2,1)}) %all-reduce.6.cloned.1.call-update) | async-done | bytes 262160 | tf_op jit(solution)/shard_map/while/body/eval_jaxpr/psum | solution.py:9
  1785.9 115.5 %all-reduce.6.cloned.1.call-done = bf16[512,256]{1,0:T(8,128)(2,1)} async-done(((bf16[512,256]{1,0:T(8,128)(2,1)}), bf16[512,256]{1,0:T(8,128)(2,1)}) %all-reduce.6.cloned.1.call-update) | async-done | bytes 262160 | tf_op jit(solution)/shard_map/while/body/eval_jaxpr/psum | solution.py:9
  1910.4 115.5 %all-reduce.6.cloned.1.call-done = bf16[512,256]{1,0:T(8,128)(2,1)} async-done(((bf16[512,256]{1,0:T(8,128)(2,1)}), bf16[512,256]{1,0:T(8,128)(2,1)}) %all-reduce.6.cloned.1.call-update) | async-done | bytes 262160 | tf_op jit(solution)/shard_map/while/body/eval_jaxpr/psum | solution.py:9
  2029.1 1.6 fusion.6
  2030.8 108.2 %all-reduce.4.cloned.1.call-done = bf16[1024,1024]{1,0:T(8,128)(2,1)} async-done(((bf16[1024,1024]{1,0:T(8,128)(2,1)}), bf16[1024,1024]{1,0:T(8,128)(2,1)}) %all-reduce.4.cloned.1.call-update) | async-done | bytes 2097168 | tf_op jit(solution)/shard_map/psum | solution.py:120
  2139.0 1.8 convert_multiply_fusion
  (167 shorter events, 94.9 us)
Async XLA Ops:
  20.0 125.2 %all-reduce.6.cloned.1.call-start = ((), (), s32[]{:S(2)}) async-start(), calls=%async_computation.1 | async-start | bytes 524288 | tf_op jit(solution)/shard_map/while/body/eval_jaxpr/psum | solution.py:9
  148.8 122.6 %all-reduce.6.cloned.1.call-start = ((), (), s32[]{:S(2)}) async-start(), calls=%async_computation.1 | async-start | bytes 524288 | tf_op jit(solution)/shard_map/while/body/eval_jaxpr/psum | solution.py:9
  275.1 122.6 %all-reduce.6.cloned.1.call-start = ((), (), s32[]{:S(2)}) async-start(), calls=%async_computation.1 | async-start | bytes 524288 | tf_op jit(solution)/shard_map/while/body/eval_jaxpr/psum | solution.py:9
  401.3 122.3 %all-reduce.6.cloned.1.call-start = ((), (), s32[]{:S(2)}) async-start(), calls=%async_computation.1 | async-start | bytes 524288 | tf_op jit(solution)/shard_map/while/body/eval_jaxpr/psum | solution.py:9
  527.2 122.3 %all-reduce.6.cloned.1.call-start = ((), (), s32[]{:S(2)}) async-start(), calls=%async_computation.1 | async-start | bytes 524288 | tf_op jit(solution)/shard_map/while/body/eval_jaxpr/psum | solution.py:9
  651.7 125.9 %all-reduce.6.cloned.1.call-start = ((), (), s32[]{:S(2)}) async-start(), calls=%async_computation.1 | async-start | bytes 524288 | tf_op jit(solution)/shard_map/while/body/eval_jaxpr/psum | solution.py:9
  779.8 122.6 %all-reduce.6.cloned.1.call-start = ((), (), s32[]{:S(2)}) async-start(), calls=%async_computation.1 | async-start | bytes 524288 | tf_op jit(solution)/shard_map/while/body/eval_jaxpr/psum | solution.py:9
  904.6 123.7 %all-reduce.6.cloned.1.call-start = ((), (), s32[]{:S(2)}) async-start(), calls=%async_computation.1 | async-start | bytes 524288 | tf_op jit(solution)/shard_map/while/body/eval_jaxpr/psum | solution.py:9
  1030.5 122.6 %all-reduce.6.cloned.1.call-start = ((), (), s32[]{:S(2)}) async-start(), calls=%async_computation.1 | async-start | bytes 524288 | tf_op jit(solution)/shard_map/while/body/eval_jaxpr/psum | solution.py:9
  1155.3 123.0 %all-reduce.6.cloned.1.call-start = ((), (), s32[]{:S(2)}) async-start(), calls=%async_computation.1 | async-start | bytes 524288 | tf_op jit(solution)/shard_map/while/body/eval_jaxpr/psum | solution.py:9
  1280.5 122.6 %all-reduce.6.cloned.1.call-start = ((), (), s32[]{:S(2)}) async-start(), calls=%async_computation.1 | async-start | bytes 524288 | tf_op jit(solution)/shard_map/while/body/eval_jaxpr/psum | solution.py:9
  1405.3 122.3 %all-reduce.6.cloned.1.call-start = ((), (), s32[]{:S(2)}) async-start(), calls=%async_computation.1 | async-start | bytes 524288 | tf_op jit(solution)/shard_map/while/body/eval_jaxpr/psum | solution.py:9
  1529.8 122.6 %all-reduce.6.cloned.1.call-start = ((), (), s32[]{:S(2)}) async-start(), calls=%async_computation.1 | async-start | bytes 524288 | tf_op jit(solution)/shard_map/while/body/eval_jaxpr/psum | solution.py:9
  1654.6 122.3 %all-reduce.6.cloned.1.call-start = ((), (), s32[]{:S(2)}) async-start(), calls=%async_computation.1 | async-start | bytes 524288 | tf_op jit(solution)/shard_map/while/body/eval_jaxpr/psum | solution.py:9
  1779.1 122.3 %all-reduce.6.cloned.1.call-start = ((), (), s32[]{:S(2)}) async-start(), calls=%async_computation.1 | async-start | bytes 524288 | tf_op jit(solution)/shard_map/while/body/eval_jaxpr/psum | solution.py:9
  1903.6 122.3 %all-reduce.6.cloned.1.call-start = ((), (), s32[]{:S(2)}) async-start(), calls=%async_computation.1 | async-start | bytes 524288 | tf_op jit(solution)/shard_map/while/body/eval_jaxpr/psum | solution.py:9
  2028.1 2.7 copy-start
  2028.1 110.9 %all-reduce.4.cloned.1.call-start = ((), (), s32[]{:S(2)}) async-start(), calls=%async_computation | async-start | bytes 4194304 | tf_op jit(solution)/shard_map/psum | solution.py:120
Sparse Core Ops, SparseCore 0:
  23.8 121.3 all-reduce.5
  152.7 118.7 all-reduce.5
  278.9 118.7 all-reduce.5
  404.8 118.7 all-reduce.5
  532.9 116.5 all-reduce.5
  655.3 122.3 all-reduce.5
  783.7 118.7 all-reduce.5
  908.5 119.7 all-reduce.5
  1034.4 118.7 all-reduce.5
  1158.9 119.4 all-reduce.5
  1284.4 118.7 all-reduce.5
  1408.8 118.7 all-reduce.5
  1533.7 118.7 all-reduce.5
  1658.1 118.7 all-reduce.5
  1782.6 118.7 all-reduce.5
  1907.1 118.7 all-reduce.5
Sparse Core Ops, SparseCore 1:
  2031.1 107.9 all-reduce.3
where the time goes:
time: 2150 us
  waiting for transfers between devices  1960 us (91%)
  other arithmetic  58.1 us (3%)
  loops' own time  54.4 us (3%)
  local copies, waits for them, and re-layouts  46.2 us (2%)
    psum x16, waiting for transfers between devices, from_root(): return lax.psum(block, axis)  1860 us
    psum x1, waiting for transfers between devices, on_device(): total = lax.psum(gram_tile.astype(jnp.bfloat16), 'dp').astype(jnp.float32)  108 us
    another operation x1, loops' own time, on_device(): lax.fori_loop(0, block_count, turn, (residual, solved, first_tile, second...  54.1 us
  transfers between devices with their start and end apart: 17, of which 17 were waited for; matrix products, arithmetic and copies ran while one was open for 1% of the time, Pallas kernels for 0%

commit v1 on v0

--- a/solution.py
+++ b/solution.py
@@ -117,7 +117,9 @@
     bottom_rows = jnp.concatenate([lower_left, jnp.tril(lower_right)], 1)
     gram_tile = jnp.concatenate([top_rows, bottom_rows], 0)
     scale = 1.0 / (points * lax.axis_size("dp"))
-    total = lax.psum(gram_tile.astype(jnp.bfloat16), "dp").astype(jnp.float32)
+    total = jnp.sum(lax.all_gather(gram_tile.astype(jnp.bfloat16), "dp"), axis=0).astype(
+        jnp.float32
+    )
     share_rows = total.shape[0] // lax.axis_size("dp")
     gram = lax.dynamic_slice_in_dim(total, lax.axis_index("dp") * share_rows, share_rows, 0)
     return (solved.reshape(slot_count * width, points), gram * scale)

time: 2150 us -> 2220 us (1.033)
  waiting for transfers between devices: 1960 us -> 2050 us
    all_gather x0 -> x1, waiting for transfers between devices: none -> 183 us  [on_device(): lax.all_gather(gram_tile.astype(jnp.bfloat16), 'dp')]
    psum x1 -> x0, waiting for transfers between devices: 108 us -> none  [on_device(): total = lax.psum(gram_tile.astype(jnp.bfloat16), 'dp').astype(jnp.float32)]
  transfers between devices with their start and end apart: 17 -> 17, of which waited for: 17 -> 17; matrix products, arithmetic and copies ran while one was open for 1% -> 0% of each run, Pallas kernels for 0% -> 0%
where the time goes in v1:
time: 2220 us
  waiting for transfers between devices  2050 us (92%)
  loops' own time  53.8 us (2%)
  other arithmetic  51.8 us (2%)
  local copies, waits for them, and re-layouts  34.7 us (2%)
    psum x16, waiting for transfers between devices, from_root(): return lax.psum(block, axis)  1870 us
    all_gather x1, waiting for transfers between devices, on_device(): lax.all_gather(gram_tile.astype(jnp.bfloat16), 'dp')  183 us
    another operation x1, loops' own time, on_device(): lax.fori_loop(0, block_count, turn, (residual, solved, first_tile, second...  53.5 us
  transfers between devices with their start and end apart: 17, of which 17 were waited for; matrix products, arithmetic and copies ran while one was open for 0% of the time, Pallas kernels for 0%

profile of v1, /device:TPU:0, one launch (start us, length us, event | category | flops | bytes accessed | tf_op | source)
XLA Modules:
  0.0 2217.3 jit_solution(14180343333692520505)
XLA Ops:
  8.0 1.6 fusion.11
  13.0 6.7 subtract_bitcast_fusion
  19.8 1994.0 %while.22 = (s32[]{:T(128)}, f32[1,512,256]{2,1,0:T(8,128)S(1)}, bf16[1,512,256]{2,1,0:T(8,128)(2,1)S(1)}, bf16[512,256]{1,0:T(8,128)(2,1)S(1)}, bf16[512,256]{1...) while((s32[]{:T(128)}, f32[1,512,256]{2,1,0:T(8,128)S(1)}, ...), condition=%wide.region_7.8_spmd.clone, body=%wide.region_1.7_spmd.clone.sunk | while | flops 940834816 | bytes 8913397 | solution.py:103
  25.8 119.2 %all-reduce.3.cloned.1.call-done = bf16[512,256]{1,0:T(8,128)(2,1)} async-done(((bf16[512,256]{1,0:T(8,128)(2,1)}), bf16[512,256]{1,0:T(8,128)(2,1)}) %all-reduce.3.cloned.1.call-update) | async-done | bytes 262160 | tf_op jit(solution)/shard_map/while/body/eval_jaxpr/psum | solution.py:9
  145.1 1.5 conditional.7
  145.1 1.5 fusion.2
  153.8 116.6 %all-reduce.3.cloned.1.call-done = bf16[512,256]{1,0:T(8,128)(2,1)} async-done(((bf16[512,256]{1,0:T(8,128)(2,1)}), bf16[512,256]{1,0:T(8,128)(2,1)}) %all-reduce.3.cloned.1.call-update) | async-done | bytes 262160 | tf_op jit(solution)/shard_map/while/body/eval_jaxpr/psum | solution.py:9
  270.4 1.5 conditional.7
  270.4 1.5 fusion.2
  279.2 116.6 %all-reduce.3.cloned.1.call-done = bf16[512,256]{1,0:T(8,128)(2,1)} async-done(((bf16[512,256]{1,0:T(8,128)(2,1)}), bf16[512,256]{1,0:T(8,128)(2,1)}) %all-reduce.3.cloned.1.call-update) | async-done | bytes 262160 | tf_op jit(solution)/shard_map/while/body/eval_jaxpr/psum | solution.py:9
  395.7 1.5 conditional.7
  395.7 1.5 fusion.2
  404.5 116.3 %all-reduce.3.cloned.1.call-done = bf16[512,256]{1,0:T(8,128)(2,1)} async-done(((bf16[512,256]{1,0:T(8,128)(2,1)}), bf16[512,256]{1,0:T(8,128)(2,1)}) %all-reduce.3.cloned.1.call-update) | async-done | bytes 262160 | tf_op jit(solution)/shard_map/while/body/eval_jaxpr/psum | solution.py:9
  520.8 1.5 conditional.7
  520.8 1.5 fusion.2
  526.1 2.2 conditional.6
  526.1 2.2 convolution_convert_fusion
  531.7 114.1 %all-reduce.3.cloned.1.call-done = bf16[512,256]{1,0:T(8,128)(2,1)} async-done(((bf16[512,256]{1,0:T(8,128)(2,1)}), bf16[512,256]{1,0:T(8,128)(2,1)}) %all-reduce.3.cloned.1.call-update) | async-done | bytes 262160 | tf_op jit(solution)/shard_map/while/body/eval_jaxpr/psum | solution.py:9
  653.1 119.9 %all-reduce.3.cloned.1.call-done = bf16[512,256]{1,0:T(8,128)(2,1)} async-done(((bf16[512,256]{1,0:T(8,128)(2,1)}), bf16[512,256]{1,0:T(8,128)(2,1)}) %all-reduce.3.cloned.1.call-update) | async-done | bytes 262160 | tf_op jit(solution)/shard_map/while/body/eval_jaxpr/psum | solution.py:9
  780.3 116.6 %all-reduce.3.cloned.1.call-done = bf16[512,256]{1,0:T(8,128)(2,1)} async-done(((bf16[512,256]{1,0:T(8,128)(2,1)}), bf16[512,256]{1,0:T(8,128)(2,1)}) %all-reduce.3.cloned.1.call-update) | async-done | bytes 262160 | tf_op jit(solution)/shard_map/while/body/eval_jaxpr/psum | solution.py:9
  904.3 117.6 %all-reduce.3.cloned.1.call-done = bf16[512,256]{1,0:T(8,128)(2,1)} async-done(((bf16[512,256]{1,0:T(8,128)(2,1)}), bf16[512,256]{1,0:T(8,128)(2,1)}) %all-reduce.3.cloned.1.call-update) | async-done | bytes 262160 | tf_op jit(solution)/shard_map/while/body/eval_jaxpr/psum | solution.py:9
  1029.3 116.6 %all-reduce.3.cloned.1.call-done = bf16[512,256]{1,0:T(8,128)(2,1)} async-done(((bf16[512,256]{1,0:T(8,128)(2,1)}), bf16[512,256]{1,0:T(8,128)(2,1)}) %all-reduce.3.cloned.1.call-update) | async-done | bytes 262160 | tf_op jit(solution)/shard_map/while/body/eval_jaxpr/psum | solution.py:9
  1153.2 117.0 %all-reduce.3.cloned.1.call-done = bf16[512,256]{1,0:T(8,128)(2,1)} async-done(((bf16[512,256]{1,0:T(8,128)(2,1)}), bf16[512,256]{1,0:T(8,128)(2,1)}) %all-reduce.3.cloned.1.call-update) | async-done | bytes 262160 | tf_op jit(solution)/shard_map/while/body/eval_jaxpr/psum | solution.py:9
  1277.5 116.6 %all-reduce.3.cloned.1.call-done = bf16[512,256]{1,0:T(8,128)(2,1)} async-done(((bf16[512,256]{1,0:T(8,128)(2,1)}), bf16[512,256]{1,0:T(8,128)(2,1)}) %all-reduce.3.cloned.1.call-update) | async-done | bytes 262160 | tf_op jit(solution)/shard_map/while/body/eval_jaxpr/psum | solution.py:9
  1401.4 116.3 %all-reduce.3.cloned.1.call-done = bf16[512,256]{1,0:T(8,128)(2,1)} async-done(((bf16[512,256]{1,0:T(8,128)(2,1)}), bf16[512,256]{1,0:T(8,128)(2,1)}) %all-reduce.3.cloned.1.call-update) | async-done | bytes 262160 | tf_op jit(solution)/shard_map/while/body/eval_jaxpr/psum | solution.py:9
  1525.0 116.6 %all-reduce.3.cloned.1.call-done = bf16[512,256]{1,0:T(8,128)(2,1)} async-done(((bf16[512,256]{1,0:T(8,128)(2,1)}), bf16[512,256]{1,0:T(8,128)(2,1)}) %all-reduce.3.cloned.1.call-update) | async-done | bytes 262160 | tf_op jit(solution)/shard_map/while/body/eval_jaxpr/psum | solution.py:9
  1649.0 116.3 %all-reduce.3.cloned.1.call-done = bf16[512,256]{1,0:T(8,128)(2,1)} async-done(((bf16[512,256]{1,0:T(8,128)(2,1)}), bf16[512,256]{1,0:T(8,128)(2,1)}) %all-reduce.3.cloned.1.call-update) | async-done | bytes 262160 | tf_op jit(solution)/shard_map/while/body/eval_jaxpr/psum | solution.py:9
  1772.6 116.3 %all-reduce.3.cloned.1.call-done = bf16[512,256]{1,0:T(8,128)(2,1)} async-done(((bf16[512,256]{1,0:T(8,128)(2,1)}), bf16[512,256]{1,0:T(8,128)(2,1)}) %all-reduce.3.cloned.1.call-update) | async-done | bytes 262160 | tf_op jit(solution)/shard_map/while/body/eval_jaxpr/psum | solution.py:9
  1896.2 116.3 %all-reduce.3.cloned.1.call-done = bf16[512,256]{1,0:T(8,128)(2,1)} async-done(((bf16[512,256]{1,0:T(8,128)(2,1)}), bf16[512,256]{1,0:T(8,128)(2,1)}) %all-reduce.3.cloned.1.call-update) | async-done | bytes 262160 | tf_op jit(solution)/shard_map/while/body/eval_jaxpr/psum | solution.py:9
  2015.2 1.5 pad_maximum_fusion
  2016.7 183.2 %all-gather.2.cloned.1.call-done = bf16[8,1024,1024]{2,1,0:T(8,128)(2,1)} async-done(((bf16[1,1024,1024]{2,1,0:T(8,128)(2,1)}), bf16[8,1024,1024]{2,1,0:T(8,128)(2,1)}) %all-gather.2.cloned.1.call-update) | async-done | bytes 16777232 | tf_op jit(solution)/shard_map/all_gather | solution.py:120
  2199.9 9.5 reduce_sum.25
  (233 shorter events, 69.7 us)
Async XLA Ops:
  19.8 4.1 copy-start.2
  19.8 125.3 %all-reduce.3.cloned.1.call-start = ((), (), s32[]{:S(2)}) async-start(), calls=%async_computation.1 | async-start | bytes 524288 | tf_op jit(solution)/shard_map/while/body/eval_jaxpr/psum | solution.py:9
  147.8 4.1 copy-start.2
  147.8 122.6 %all-reduce.3.cloned.1.call-start = ((), (), s32[]{:S(2)}) async-start(), calls=%async_computation.1 | async-start | bytes 524288 | tf_op jit(solution)/shard_map/while/body/eval_jaxpr/psum | solution.py:9
  273.1 4.1 copy-start.2
  273.1 122.6 %all-reduce.3.cloned.1.call-start = ((), (), s32[]{:S(2)}) async-start(), calls=%async_computation.1 | async-start | bytes 524288 | tf_op jit(solution)/shard_map/while/body/eval_jaxpr/psum | solution.py:9
  398.4 4.1 copy-start.2
  398.5 122.3 %all-reduce.3.cloned.1.call-start = ((), (), s32[]{:S(2)}) async-start(), calls=%async_computation.1 | async-start | bytes 524288 | tf_op jit(solution)/shard_map/while/body/eval_jaxpr/psum | solution.py:9
  523.5 6.3 copy-start.2
  523.5 122.3 %all-reduce.3.cloned.1.call-start = ((), (), s32[]{:S(2)}) async-start(), calls=%async_computation.1 | async-start | bytes 524288 | tf_op jit(solution)/shard_map/while/body/eval_jaxpr/psum | solution.py:9
  647.1 4.1 copy-start.2
  647.1 125.9 %all-reduce.3.cloned.1.call-start = ((), (), s32[]{:S(2)}) async-start(), calls=%async_computation.1 | async-start | bytes 524288 | tf_op jit(solution)/shard_map/while/body/eval_jaxpr/psum | solution.py:9
  774.3 4.1 copy-start.2
  774.3 122.6 %all-reduce.3.cloned.1.call-start = ((), (), s32[]{:S(2)}) async-start(), calls=%async_computation.1 | async-start | bytes 524288 | tf_op jit(solution)/shard_map/while/body/eval_jaxpr/psum | solution.py:9
  898.2 4.1 copy-start.2
  898.2 123.7 %all-reduce.3.cloned.1.call-start = ((), (), s32[]{:S(2)}) async-start(), calls=%async_computation.1 | async-start | bytes 524288 | tf_op jit(solution)/shard_map/while/body/eval_jaxpr/psum | solution.py:9
  1023.2 4.1 copy-start.2
  1023.2 122.6 %all-reduce.3.cloned.1.call-start = ((), (), s32[]{:S(2)}) async-start(), calls=%async_computation.1 | async-start | bytes 524288 | tf_op jit(solution)/shard_map/while/body/eval_jaxpr/psum | solution.py:9
  1147.1 4.1 copy-start.2
  1147.1 123.0 %all-reduce.3.cloned.1.call-start = ((), (), s32[]{:S(2)}) async-start(), calls=%async_computation.1 | async-start | bytes 524288 | tf_op jit(solution)/shard_map/while/body/eval_jaxpr/psum | solution.py:9
  1271.4 4.1 copy-start.2
  1271.5 122.6 %all-reduce.3.cloned.1.call-start = ((), (), s32[]{:S(2)}) async-start(), calls=%async_computation.1 | async-start | bytes 524288 | tf_op jit(solution)/shard_map/while/body/eval_jaxpr/psum | solution.py:9
  1395.4 4.1 copy-start.2
  1395.4 122.3 %all-reduce.3.cloned.1.call-start = ((), (), s32[]{:S(2)}) async-start(), calls=%async_computation.1 | async-start | bytes 524288 | tf_op jit(solution)/shard_map/while/body/eval_jaxpr/psum | solution.py:9
  1519.0 4.1 copy-start.2
  1519.0 122.6 %all-reduce.3.cloned.1.call-start = ((), (), s32[]{:S(2)}) async-start(), calls=%async_computation.1 | async-start | bytes 524288 | tf_op jit(solution)/shard_map/while/body/eval_jaxpr/psum | solution.py:9
  1642.9 4.1 copy-start.2
  1642.9 122.3 %all-reduce.3.cloned.1.call-start = ((), (), s32[]{:S(2)}) async-start(), calls=%async_computation.1 | async-start | bytes 524288 | tf_op jit(solution)/shard_map/while/body/eval_jaxpr/psum | solution.py:9
  1766.6 4.1 copy-start.2
  1766.6 122.3 %all-reduce.3.cloned.1.call-start = ((), (), s32[]{:S(2)}) async-start(), calls=%async_computation.1 | async-start | bytes 524288 | tf_op jit(solution)/shard_map/while/body/eval_jaxpr/psum | solution.py:9
  1890.2 122.3 %all-reduce.3.cloned.1.call-start = ((), (), s32[]{:S(2)}) async-start(), calls=%async_computation.1 | async-start | bytes 524288 | tf_op jit(solution)/shard_map/while/body/eval_jaxpr/psum | solution.py:9
  2013.8 186.1 %all-gather.2.cloned.1.call-start = ((), (), s32[]{:S(2)}) async-start(), calls=%async_computation | async-start | bytes 18874368 | tf_op jit(solution)/shard_map/all_gather | solution.py:120
  (18 other events, 29.2 us)
Sparse Core Ops, SparseCore 0:
  23.7 121.3 all-reduce.2
  151.6 118.7 all-reduce.2
  277.0 118.7 all-reduce.2
  402.0 118.7 all-reduce.2
  529.2 116.5 all-reduce.2
  650.6 122.3 all-reduce.2
  778.2 118.7 all-reduce.2
  902.1 119.7 all-reduce.2
  1027.1 118.7 all-reduce.2
  1150.7 119.4 all-reduce.2
  1275.3 118.7 all-reduce.2
  1398.9 118.7 all-reduce.2
  1522.9 118.7 all-reduce.2
  1646.5 118.7 all-reduce.2
  1770.1 118.7 all-reduce.2
  1893.7 118.7 all-reduce.2
Sparse Core Ops, SparseCore 1:
  2016.8 183.1 all-gather.1
